TPU v7x, 512 devices: a whole 4x4x16 slice. The times are simulated.
512 devices in a mesh: gx: 16 (over x, z_hi, core), gy: 32 (over z_lo, y).
Axes of the slice: x: 4, y: 4, z: 16 (z_hi: 2, z_lo: 8; z = z_hi * 8 + z_lo), core: 2. Of those that a mesh axis runs over, the one named last changes fastest.
Arguments:
- fine_multipoles: bfloat16 [32, 32, 32, 2, 256], P('gx', 'gy'), may hold values from -6 to 6
- m2m_ops: bfloat16 [2, 2, 2, 256, 256], replicated, may hold values from -0.125 to 0.125
- m2l_ops: bfloat16 [512, 256, 256], P('gy'), may hold values from -0.015625 to 0.015625
- offsets: int32 [512, 3], P('gy'), may hold values from -7 to 7, as said below
Outputs:
- local_expansions: float32 [16, 256, 2, 256], P('gx', 'gy')
Inputs may be any that keep to these rules, and one draw needn't show every extreme that they name: Rows are distinct offsets; the first component lies in -3 to 3; in each row the largest magnitude of the three components is 2 or more.
All inputs are finite; a program needn't handle non-finite values.
Results may differ from a plain program's by a relative error of at most 0.0029.
Values may be sent and summed in bfloat16 or wider, within the bound.
A program may use at most 64 MiB of HBM per device.

v0:
```python
import jax
import jax.numpy as jnp
from jax import lax
from jax.sharding import PartitionSpec as P


def from_partner(array, axis, stride):
    return lax.ppermute(array, axis, [(i, i ^ 1 << stride) for i in range(lax.axis_size(axis))])


def passed_along(value, axis, steps):
    count = lax.axis_size(axis)
    pairs = [(source, (source + steps) % count) for source in range(count)]
    return lax.ppermute(value, axis, pairs)


def on_device(fine_multipoles, m2m_ops, m2l_ops, offsets):
    fine_boxes = fine_multipoles.shape[2]
    charge_sets = fine_multipoles.shape[3]
    coeffs = fine_multipoles.shape[4]
    half_z = fine_boxes // 2
    quarter = half_z // 2
    y_index = lax.axis_index("gy")
    parity = y_index % 2
    selected = lax.dynamic_index_in_dim(m2m_ops, parity, 1, keepdims=False)
    children = fine_multipoles[:, 0].reshape(2, half_z, 2, charge_sets, coeffs)
    partial_value = jnp.einsum(
        "azcri,acio->zro", children, selected, preferred_element_type=jnp.float32
    )
    kept_half = lax.dynamic_slice_in_dim(partial_value, parity * quarter, quarter, 0)
    sent_half = lax.dynamic_slice_in_dim(partial_value, (1 - parity) * quarter, quarter, 0)
    arrived = from_partner(sent_half, "gy", 0)
    coarse_mine = (kept_half + arrived).astype(jnp.bfloat16)
    slab_boxes = lax.all_gather(coarse_mine, "gy", axis=0, tiled=True)
    ahead_planes = [passed_along(slab_boxes, "gx", -distance) for distance in (1, 2, 3)]
    behind_planes = [passed_along(slab_boxes, "gx", distance) for distance in (1, 2, 3)]
    stacked = jnp.stack(behind_planes[::-1] + [slab_boxes] + ahead_planes)
    coarse_rows = slab_boxes.shape[0] // half_z
    plane_grid = stacked.reshape(7, coarse_rows, half_z, charge_sets, coeffs)
    count_ops = m2l_ops.shape[0]
    sources = []
    for op_entry in range(count_ops):
        shift_row = offsets[op_entry]
        chosen_plane = lax.dynamic_index_in_dim(plane_grid, shift_row[0] + 3, 0, keepdims=False)
        rolled = jnp.roll(chosen_plane, (-shift_row[1], -shift_row[2]), axis=(0, 1))
        sources.append(rolled.reshape(coarse_rows * half_z, charge_sets, coeffs))
    summed = jnp.zeros((quarter * lax.axis_size("gy") * charge_sets, coeffs), jnp.float32)
    for op_entry in range(count_ops):
        row_block = sources[op_entry].reshape(quarter * lax.axis_size("gy") * charge_sets, coeffs)
        summed = summed + jnp.dot(row_block, m2l_ops[op_entry], preferred_element_type=jnp.float32)
    my_locals = lax.psum_scatter(
        summed.reshape(quarter * lax.axis_size("gy"), charge_sets, coeffs),
        "gy",
        scatter_dimension=0,
        tiled=True,
    )
    return my_locals[None]


def solution(mesh):
    return jax.shard_map(
        on_device,
        mesh=mesh,
        in_specs=(P("gx", "gy", None, None, None), P(), P("gy", None, None), P("gy", None)),
        out_specs=P("gx", "gy", None, None),
        check_vma=False,
    )
```

profile of v0, /device:TPU:2, one launch (start us, length us, event | category | flops | bytes accessed | tf_op | source)
XLA Modules:
  0.0 762.5 jit_solution(14882671886684901363)
XLA Ops:
  6.5 1.2 copy-done
  7.8 1.0 convolution_bitcast_fusion
  8.8 3.5 collective-permute-start
  12.3 2.1 collective-permute-done
  14.5 127.3 %all_gather.3 = bf16[256,2,256]{2,0,1:T(8,128)(2,1)S(1)} all-gather(bf16[8,2,256]{2,0,1:T(8,128)(2,1)S(1)} %fusion.71), channel_id=1, replica_groups=mesh['gx'=16,'gy'=32] {'gy'}, dimensions={0}, use_global_device_ids=true | all-gather | bytes 270336 | tf_op jit(solution)/shard_map/all_gather | solution.py:34
  141.8 1.9 collective-permute-start.1
  143.7 2.1 fusion.73
  148.5 2.1 fusion.74
  163.8 8.3 %collective-permute-start.2 = (bf16[256,2,256]{2,0,1:T(8,128)(2,1)S(1)}, bf16[256,2,256]{2,0,1:T(8,128)(2,1)S(1)}, u32[]{:S(2)}, u32[]{:S(2)}) collective-permute-start(bf16[256,2,256]{2,0,1:T(8,128)(2,1)S(1)} %all_gather.3), channel_id=1, source_target_pairs={{0,64},{32,96},{64,128},{96,160},{128,192},{160,224},{192,256},{22... | collective-permute-start | bytes 786440 | tf_op jit(solution)/shard_map/ppermute | solution.py:14
  172.1 1.7 fusion.75
  183.4 3.3 collective-permute-start.3
  201.7 11.9 %collective-permute-start.4 = (bf16[256,2,256]{2,0,1:T(8,128)(2,1)S(1)}, bf16[256,2,256]{2,0,1:T(8,128)(2,1)S(1)}, u32[]{:S(2)}, u32[]{:S(2)}) collective-permute-start(bf16[256,2,256]{2,0,1:T(8,128)(2,1)S(1)} %all_gather.3), channel_id=1, source_target_pairs={{0,480},{32,0},{64,32},{96,64},{128,96},{160,128},{192,160},{224,1... | collective-permute-start | bytes 786440 | tf_op jit(solution)/shard_map/ppermute | solution.py:14
  213.6 6.3 collective-permute-start.5
  219.9 2.1 collective-permute-start.6
  222.1 1.9 collective-permute-done.4
  224.0 7.5 collective-permute-done.5
  231.5 4.8 collective-permute-done.6
  236.3 1.5 constant_dynamic-slice_fusion
  237.8 1.2 copy_bitcast_fusion
  239.7 0.7 fusion.4
  240.4 0.8 reshape_reshape.62
  241.2 2.3 copy_bitcast_fusion.2
  244.1 0.7 fusion.6
  244.9 0.8 reshape_reshape.61
  245.7 1.6 fusion.9
  247.3 0.7 fusion.8
  248.0 0.8 reshape_reshape.60
  248.8 2.3 copy_bitcast_fusion.4
  251.8 0.7 fusion.10
  252.5 0.8 reshape_reshape.59
  253.3 1.6 fusion.13
  255.0 0.7 fusion.12
  255.7 0.8 reshape_reshape.58
  256.5 2.3 copy_bitcast_fusion.6
  259.5 1.0 fusion.14
  260.4 0.8 reshape_reshape.57
  261.2 1.6 fusion.17
  262.8 0.7 fusion.16
  263.6 0.8 reshape_reshape.56
  264.4 1.3 copy_bitcast_fusion.8
  266.3 0.7 fusion.18
  267.1 0.8 reshape_reshape.55
  267.9 1.6 fusion.21
  269.5 0.7 fusion.20
  270.2 0.8 reshape_reshape.54
  273.0 0.8 reshape_reshape.53
  275.2 0.8 reshape_reshape.52
  278.0 0.8 reshape_reshape.51
  278.8 0.9 fusion.29
  280.5 0.8 reshape_reshape.50
  281.3 1.3 copy_bitcast_fusion.14
  283.9 0.8 reshape_reshape.49
  284.7 1.6 fusion.33
  286.4 1.5 fusion.32
  287.8 1.1 reshape_reshape.48
  288.9 1.6 fusion.3
  290.5 1.5 fusion.2
  292.0 1.8 reshape_reshape.63
  294.0 1.2 convolution_add_fusion.14
  299.4 1.1 convolution_add_fusion
  300.5 1.1 reshape.242
  301.6 1.3 dynamic-slice.8
  303.6 450.8 %all-reduce.3.cloned.1.call-done = f32[256,2,256]{2,1,0:T(2,128)} async-done(((f32[256,2,256]{2,1,0:T(2,128)}), f32[256,2,256]{2,1,0:T(2,128)}) %all-reduce.3.cloned.1.call-update) | async-done | bytes 524304
  754.3 1.3 dynamic-slice_bitcast_fusion
  (75 shorter events, 15.2 us)
Async XLA Ops:
  6.5 1.2 copy-start
  6.5 747.8 %all-reduce.3.cloned.1.call-start = ((), (), s32[]{:S(2)}) async-start(), calls=%async_computation | async-start | bytes 1048576
  8.8 5.6 collective-permute-start
  141.8 78.1 %collective-permute-start.1 = (bf16[256,2,256]{2,0,1:T(8,128)(2,1)S(1)}, bf16[256,2,256]{2,0,1:T(8,128)(2,1)S(1)}, u32[]{:S(2)}, u32[]{:S(2)}) collective-permute-start(bf16[256,2,256]{2,0,1:T(8,128)(2,1)S(1)} %all_gather.3), channel_id=1, source_target_pairs={{0,96},{32,128},{64,160},{96,192},{128,224},{160,256},{192,288},{2... | collective-permute-start | bytes 786440 | tf_op jit(solution)/shard_map/ppermute | solution.py:14
  163.8 58.2 %collective-permute-start.2 = (bf16[256,2,256]{2,0,1:T(8,128)(2,1)S(1)}, bf16[256,2,256]{2,0,1:T(8,128)(2,1)S(1)}, u32[]{:S(2)}, u32[]{:S(2)}) collective-permute-start(bf16[256,2,256]{2,0,1:T(8,128)(2,1)S(1)} %all_gather.3), channel_id=1, source_target_pairs={{0,64},{32,96},{64,128},{96,160},{128,192},{160,224},{192,256},{22... | collective-permute-start | bytes 786440 | tf_op jit(solution)/shard_map/ppermute | solution.py:14
  183.4 38.7 %collective-permute-start.3 = (bf16[256,2,256]{2,0,1:T(8,128)(2,1)S(1)}, bf16[256,2,256]{2,0,1:T(8,128)(2,1)S(1)}, u32[]{:S(2)}, u32[]{:S(2)}) collective-permute-start(bf16[256,2,256]{2,0,1:T(8,128)(2,1)S(1)} %all_gather.3), channel_id=1, source_target_pairs={{0,32},{32,64},{64,96},{96,128},{128,160},{160,192},{192,224},{224... | collective-permute-start | bytes 786440 | tf_op jit(solution)/shard_map/ppermute | solution.py:14
  201.7 22.3 %collective-permute-start.4 = (bf16[256,2,256]{2,0,1:T(8,128)(2,1)S(1)}, bf16[256,2,256]{2,0,1:T(8,128)(2,1)S(1)}, u32[]{:S(2)}, u32[]{:S(2)}) collective-permute-start(bf16[256,2,256]{2,0,1:T(8,128)(2,1)S(1)} %all_gather.3), channel_id=1, source_target_pairs={{0,480},{32,0},{64,32},{96,64},{128,96},{160,128},{192,160},{224,1... | collective-permute-start | bytes 786440 | tf_op jit(solution)/shard_map/ppermute | solution.py:14
  213.6 17.9 %collective-permute-start.5 = (bf16[256,2,256]{2,0,1:T(8,128)(2,1)S(1)}, bf16[256,2,256]{2,0,1:T(8,128)(2,1)S(1)}, u32[]{:S(2)}, u32[]{:S(2)}) collective-permute-start(bf16[256,2,256]{2,0,1:T(8,128)(2,1)S(1)} %all_gather.3), channel_id=1, source_target_pairs={{0,448},{32,480},{64,0},{96,32},{128,64},{160,96},{192,128},{224,1... | collective-permute-start | bytes 786440 | tf_op jit(solution)/shard_map/ppermute | solution.py:14
  219.9 16.4 %collective-permute-start.6 = (bf16[256,2,256]{2,0,1:T(8,128)(2,1)S(1)}, bf16[256,2,256]{2,0,1:T(8,128)(2,1)S(1)}, u32[]{:S(2)}, u32[]{:S(2)}) collective-permute-start(bf16[256,2,256]{2,0,1:T(8,128)(2,1)S(1)} %all_gather.3), channel_id=1, source_target_pairs={{0,416},{32,448},{64,480},{96,0},{128,32},{160,64},{192,96},{224,1... | collective-permute-start | bytes 786440 | tf_op jit(solution)/shard_map/ppermute | solution.py:14
  283.2 10.5 %copy-start.1 = (bf16[16,256,256]{2,1,0:T(8,128)(2,1)S(1)}, bf16[16,256,256]{2,1,0:T(8,128)(2,1)}, u32[]{:S(2)}) copy-start(bf16[16,256,256]{2,1,0:T(8,128)(2,1)} %param.8) | copy-start | bytes 6291460
  293.7 1.5 copy-start.15
  293.7 1.7 copy-start.13
  293.9 1.7 copy-start.12
  295.2 1.0 copy-start.11
  295.4 1.0 copy-start.10
  295.7 1.0 copy-start.9
  296.1 1.0 copy-start.8
  296.4 1.0 copy-start.7
  296.7 1.0 copy-start.6
  297.1 1.0 copy-start.5
  297.4 1.0 copy-start.4
  297.7 1.0 copy-start.3
  298.1 1.0 copy-start.2
  298.4 1.0 copy-start.14
Sparse Core Ops, SparseCore 0:
  301.8 452.5 all-reduce.2
where the time goes:
time: 764 us; the launch traced here: 762 us
  waiting for transfers between devices  467 us (61%)
  blocking collectives  127 us (17%)
  between operations  55 us (7%)
  local copies, waits for them, and re-layouts  39.3 us (5%)
  starting transfers between devices  37.2 us (5%)
  other arithmetic  30.1 us (4%)
    unnamed x2, waiting for transfers between devices  451 us
    all_gather x1, blocking collectives, on_device(): slab_boxes = lax.all_gather(coarse_mine, 'gy', axis=0, tiled=True)  127 us
    ppermute x6, starting transfers between devices, passed_along(): return lax.ppermute(value, axis, pairs)  33.7 us
    concatenate x32, other arithmetic, on_device(): rolled = jnp.roll(chosen_plane, (-shift_row[1], -shift_row[2]), axis=(0, 1))  30.1 us
  transfers between devices with their start and end apart: 8, of which 5 were waited for; matrix products, arithmetic and copies ran while one was open for 1% of the time, Pallas kernels for 0%

commit v1 on v0

--- a/solution.py
+++ b/solution.py
@@ -31,7 +31,9 @@
     sent_half = lax.dynamic_slice_in_dim(partial_value, (1 - parity) * quarter, quarter, 0)
     arrived = from_partner(sent_half, "gy", 0)
     coarse_mine = (kept_half + arrived).astype(jnp.bfloat16)
-    slab_boxes = lax.all_gather(coarse_mine, "gy", axis=0, tiled=True)
+    slab_boxes = jnp.concatenate(
+        lax.all_to_all(jnp.stack([coarse_mine] * lax.axis_size("gy")), "gy", 0, 0), axis=0
+    )
     ahead_planes = [passed_along(slab_boxes, "gx", -distance) for distance in (1, 2, 3)]
     behind_planes = [passed_along(slab_boxes, "gx", distance) for distance in (1, 2, 3)]
     stacked = jnp.stack(behind_planes[::-1] + [slab_boxes] + ahead_planes)

time: 764 us -> 709 us (0.928)
  blocking collectives: 127 us -> 33.5 us
  waiting for transfers between devices: 467 us -> 492 us
  other arithmetic: 30.1 us -> 41.6 us
    all_gather x1 -> x0, blocking collectives: 127 us -> none  [on_device(): slab_boxes = lax.all_gather(coarse_mine, 'gy', axis=0, tiled=True)]
    all_to_all x0 -> x1, blocking collectives: none -> 33.5 us  [on_device(): lax.all_to_all(jnp.stack([coarse_mine] * lax.axis_size('gy')), 'gy', 0, 0)]
    ppermute x6, waiting for transfers between devices: 14.1 us -> 38.9 us  [passed_along(): return lax.ppermute(value, axis, pairs)]
    concatenate x32 -> x24, other arithmetic: 30.1 us -> 41.5 us  [on_device(): rolled = jnp.roll(chosen_plane, (-shift_row[1], -shift_row[2]), axis=(0, 1))]
where the time goes in v1:
time: 709 us; the launch traced here: 707 us
  waiting for transfers between devices  492 us (69%)
  between operations  55.2 us (8%)
  other arithmetic  41.6 us (6%)
  starting transfers between devices  39.9 us (6%)
  local copies, waits for them, and re-layouts  38.2 us (5%)
  blocking collectives  33.5 us (5%)
    unnamed x2, waiting for transfers between devices  451 us
    concatenate x24, other arithmetic, on_device(): rolled = jnp.roll(chosen_plane, (-shift_row[1], -shift_row[2]), axis=(0, 1))  41.5 us
    ppermute x6, waiting for transfers between devices, passed_along(): return lax.ppermute(value, axis, pairs)  38.9 us
    ppermute x6, starting transfers between devices, passed_along(): return lax.ppermute(value, axis, pairs)  36.4 us
    all_to_all x1, blocking collectives, on_device(): lax.all_to_all(jnp.stack([coarse_mine] * lax.axis_size('gy')), 'gy', 0, 0)  33.5 us
    another operation x16, local copies, waits for them, and re-layouts, on_device(): sources[op_entry]  19.8 us
  transfers between devices with their start and end apart: 8, of which 5 were waited for; matrix products, arithmetic and copies ran while one was open for 1% of the time, Pallas kernels for 0%

profile of v1, /device:TPU:2, one launch (start us, length us, event | category | flops | bytes accessed | tf_op | source)
XLA Modules:
  0.0 707.1 jit_solution(1501902338324950360)
XLA Ops:
  6.5 1.2 copy-done
  7.8 1.0 convolution_bitcast_fusion
  8.8 3.5 collective-permute-start
  12.3 2.1 collective-permute-done
  14.6 33.5 %all_to_all.5 = bf16[32,8,2,256]{3,2,1,0:T(2,128)(2,1)S(1)} all-to-all(bf16[32,8,2,256]{3,2,1,0:T(2,128)(2,1)S(1)} %stack.18), channel_id=1, replica_groups=mesh['gx'=16,'gy'=32] {'gy'}, dimensions={0} | all-to-all | bytes 524288 | tf_op jit(solution)/shard_map/all_to_all | solution.py:35
  48.1 4.7 collective-permute-start.1
  52.8 2.1 fusion.73
  57.5 2.1 fusion.74
  73.2 7.3 %collective-permute-start.2 = (bf16[256,2,256]{2,1,0:T(2,128)(2,1)S(1)}, bf16[256,2,256]{2,1,0:T(2,128)(2,1)S(1)}, u32[]{:S(2)}, u32[]{:S(2)}) collective-permute-start(bf16[256,2,256]{2,1,0:T(2,128)(2,1)S(1)} %bitcast.255), channel_id=1, source_target_pairs={{0,64},{32,96},{64,128},{96,160},{128,192},{160,224},{192,256},{22... | collective-permute-start | bytes 786440 | tf_op jit(solution)/shard_map/ppermute | solution.py:14
  80.5 1.7 fusion.75
  91.8 1.9 collective-permute-start.3
  108.6 13.3 %collective-permute-start.4 = (bf16[256,2,256]{2,1,0:T(2,128)(2,1)S(1)}, bf16[256,2,256]{2,1,0:T(2,128)(2,1)S(1)}, u32[]{:S(2)}, u32[]{:S(2)}) collective-permute-start(bf16[256,2,256]{2,1,0:T(2,128)(2,1)S(1)} %bitcast.257), channel_id=1, source_target_pairs={{0,480},{32,0},{64,32},{96,64},{128,96},{160,128},{192,160},{224,1... | collective-permute-start | bytes 786440 | tf_op jit(solution)/shard_map/ppermute | solution.py:14
  121.9 7.3 %collective-permute-start.5 = (bf16[256,2,256]{2,1,0:T(2,128)(2,1)S(1)}, bf16[256,2,256]{2,1,0:T(2,128)(2,1)S(1)}, u32[]{:S(2)}, u32[]{:S(2)}) collective-permute-start(bf16[256,2,256]{2,1,0:T(2,128)(2,1)S(1)} %bitcast.258), channel_id=1, source_target_pairs={{0,448},{32,480},{64,0},{96,32},{128,64},{160,96},{192,128},{224,1... | collective-permute-start | bytes 786440 | tf_op jit(solution)/shard_map/ppermute | solution.py:14
  129.2 1.9 collective-permute-start.6
  132.1 2.9 collective-permute-done.4
  135.2 31.3 %collective-permute-done.5 = bf16[256,2,256]{2,1,0:T(2,128)(2,1)S(1)} collective-permute-done((bf16[256,2,256]{2,1,0:T(2,128)(2,1)S(1)}, bf16[256,2,256]{2,1,0:T(2,128)(2,1)S(1)}, u32[]{:S(2)}, u32[]{:S(2)}) %collective-permute-start.5) | collective-permute-done | bytes 262176 | tf_op jit(solution)/shard_map/ppermute | solution.py:14
  166.7 4.7 collective-permute-done.6
  171.6 4.8 dynamic-slice_bitcast_fusion
  176.4 2.0 fusion.3
  178.4 1.4 fusion.2
  179.8 1.7 reshape_reshape.63
  181.6 2.4 fusion.4
  184.0 1.7 reshape_reshape.62
  185.7 3.1 fusion.7
  188.8 1.4 fusion.6
  190.2 1.7 reshape_reshape.61
  192.0 2.4 fusion.8
  194.4 1.8 reshape_reshape.60
  196.1 3.1 fusion.11
  199.2 1.5 fusion.10
  200.7 1.8 reshape_reshape.59
  202.4 2.4 fusion.12
  204.8 1.8 reshape_reshape.58
  206.6 2.0 fusion.15
  208.6 0.7 fusion.14
  209.3 0.8 reshape_reshape.57
  210.1 1.9 fusion.16
  212.1 0.8 reshape_reshape.56
  212.9 1.3 fusion.19
  214.2 0.7 fusion.18
  214.9 0.8 reshape_reshape.55
  215.7 0.7 fusion.20
  216.5 0.8 reshape_reshape.54
  217.3 1.3 fusion.23
  218.6 0.7 fusion.22
  219.3 0.8 reshape_reshape.53
  220.1 0.7 fusion.24
  220.9 0.8 reshape_reshape.52
  221.7 2.0 fusion.27
  223.7 0.7 fusion.26
  224.4 0.8 reshape_reshape.51
  225.2 2.5 fusion.28
  227.8 1.7 reshape_reshape.50
  229.5 3.0 fusion.31
  232.5 1.0 fusion.30
  233.5 0.8 reshape_reshape.49
  234.3 2.4 fusion.32
  236.7 1.1 reshape_reshape.48
  238.0 1.2 convolution_add_fusion.14
  243.5 1.1 convolution_add_fusion
  244.6 1.1 reshape.248
  245.7 1.3 dynamic-slice.8
  247.7 451.3 %all-reduce.3.cloned.1.call-done = f32[256,2,256]{2,1,0:T(2,128)} async-done(((f32[256,2,256]{2,1,0:T(2,128)}), f32[256,2,256]{2,1,0:T(2,128)}) %all-reduce.3.cloned.1.call-update) | async-done | bytes 524304
  698.9 1.3 dynamic-slice_bitcast_fusion.16
  (61 shorter events, 6.1 us)
Async XLA Ops:
  6.5 1.2 copy-start
  6.5 692.4 %all-reduce.3.cloned.1.call-start = ((), (), s32[]{:S(2)}) async-start(), calls=%async_computation.1 | async-start | bytes 1048576
  8.8 5.6 collective-permute-start
  48.1 81.1 %collective-permute-start.1 = (bf16[256,2,256]{2,1,0:T(2,128)(2,1)S(1)}, bf16[256,2,256]{2,1,0:T(2,128)(2,1)S(1)}, u32[]{:S(2)}, u32[]{:S(2)}) collective-permute-start(bf16[256,2,256]{2,1,0:T(2,128)(2,1)S(1)} %bitcast.254), channel_id=1, source_target_pairs={{0,96},{32,128},{64,160},{96,192},{128,224},{160,256},{192,288},{2... | collective-permute-start | bytes 786440 | tf_op jit(solution)/shard_map/ppermute | solution.py:14
  73.2 58.1 %collective-permute-start.2 = (bf16[256,2,256]{2,1,0:T(2,128)(2,1)S(1)}, bf16[256,2,256]{2,1,0:T(2,128)(2,1)S(1)}, u32[]{:S(2)}, u32[]{:S(2)}) collective-permute-start(bf16[256,2,256]{2,1,0:T(2,128)(2,1)S(1)} %bitcast.255), channel_id=1, source_target_pairs={{0,64},{32,96},{64,128},{96,160},{128,192},{160,224},{192,256},{22... | collective-permute-start | bytes 786440 | tf_op jit(solution)/shard_map/ppermute | solution.py:14
  91.8 39.8 %collective-permute-start.3 = (bf16[256,2,256]{2,1,0:T(2,128)(2,1)S(1)}, bf16[256,2,256]{2,1,0:T(2,128)(2,1)S(1)}, u32[]{:S(2)}, u32[]{:S(2)}) collective-permute-start(bf16[256,2,256]{2,1,0:T(2,128)(2,1)S(1)} %bitcast.256), channel_id=1, source_target_pairs={{0,32},{32,64},{64,96},{96,128},{128,160},{160,192},{192,224},{224... | collective-permute-start | bytes 786440 | tf_op jit(solution)/shard_map/ppermute | solution.py:14
  108.6 26.3 %collective-permute-start.4 = (bf16[256,2,256]{2,1,0:T(2,128)(2,1)S(1)}, bf16[256,2,256]{2,1,0:T(2,128)(2,1)S(1)}, u32[]{:S(2)}, u32[]{:S(2)}) collective-permute-start(bf16[256,2,256]{2,1,0:T(2,128)(2,1)S(1)} %bitcast.257), channel_id=1, source_target_pairs={{0,480},{32,0},{64,32},{96,64},{128,96},{160,128},{192,160},{224,1... | collective-permute-start | bytes 786440 | tf_op jit(solution)/shard_map/ppermute | solution.py:14
  121.9 44.5 %collective-permute-start.5 = (bf16[256,2,256]{2,1,0:T(2,128)(2,1)S(1)}, bf16[256,2,256]{2,1,0:T(2,128)(2,1)S(1)}, u32[]{:S(2)}, u32[]{:S(2)}) collective-permute-start(bf16[256,2,256]{2,1,0:T(2,128)(2,1)S(1)} %bitcast.258), channel_id=1, source_target_pairs={{0,448},{32,480},{64,0},{96,32},{128,64},{160,96},{192,128},{224,1... | collective-permute-start | bytes 786440 | tf_op jit(solution)/shard_map/ppermute | solution.py:14
  129.2 42.2 %collective-permute-start.6 = (bf16[256,2,256]{2,1,0:T(2,128)(2,1)S(1)}, bf16[256,2,256]{2,1,0:T(2,128)(2,1)S(1)}, u32[]{:S(2)}, u32[]{:S(2)}) collective-permute-start(bf16[256,2,256]{2,1,0:T(2,128)(2,1)S(1)} %bitcast.259), channel_id=1, source_target_pairs={{0,416},{32,448},{64,480},{96,0},{128,32},{160,64},{192,96},{224,1... | collective-permute-start | bytes 786440 | tf_op jit(solution)/shard_map/ppermute | solution.py:14
  225.2 12.6 %copy-start.1 = (bf16[16,256,256]{2,1,0:T(8,128)(2,1)S(1)}, bf16[16,256,256]{2,1,0:T(8,128)(2,1)}, u32[]{:S(2)}) copy-start(bf16[16,256,256]{2,1,0:T(8,128)(2,1)} %param.8) | copy-start | bytes 6291460
  237.8 1.5 copy-start.15
  237.8 1.7 copy-start.14
  238.0 1.7 copy-start.13
  239.3 1.0 copy-start.12
  239.5 1.0 copy-start.11
  239.8 1.0 copy-start.10
  240.2 1.0 copy-start.9
  240.5 1.0 copy-start.8
  240.8 1.0 copy-start.7
  241.2 1.0 copy-start.6
  241.5 1.0 copy-start.5
  241.8 1.0 copy-start.4
  242.2 1.0 copy-start.3
  242.5 1.0 copy-start.2
Sparse Core Ops, SparseCore 0:
  245.8 453.0 all-reduce.2
